TPU v7x, 256 devices: a whole 4x4x8 slice. The times are simulated.
256 devices in a mesh: child: 2 (over y_hi), row: 32 (over z, y_lo, core), col: 4 (over x).
Axes of the slice: x: 4, y: 4 (y_hi: 2, y_lo: 2; y = y_hi * 2 + y_lo), z: 8, core: 2. Of those that a mesh axis runs over, the one named last changes fastest.
Arguments:
- front: bfloat16 [131072, 2048], P(('row', 'child'), 'col'), as said below
- left_factors: bfloat16 [2, 4, 64, 131072], P('child', 'col', None, 'row'), may hold values from -2.5 to 2.5
- right_factors: bfloat16 [2, 256, 64, 2048], P('child', 'row', None, 'col'), may hold values from -2.5 to 2.5
Outputs:
- panel_t: bfloat16 [2048, 131072], P('col', ('row', 'child'))
Inputs may be any that keep to these rules, and one draw needn't show every extreme that they name: The first 2048 rows of front make the symmetric part of the assembled diagonal block positive definite: its diagonal entries exceed the spectral norm of the rest of that part several times.
All inputs are finite; a program needn't handle non-finite values.
Results may differ from a plain program's by a relative error of at most 0.012.
Values may be sent and summed in bfloat16 or wider, within the bound.
No kernel may reach another device: no remote copies, remote signals or barrier semaphores. Data moves between devices by JAX's collectives and lax.ppermute only.
A program may use at most 128 MiB of HBM per device.

v0:
```python
import jax
import jax.numpy as jnp
from jax import lax
from jax.sharding import PartitionSpec as P

TILE = 512
RANK = 64
PW = 2048


def shortened(array):

    def short(part):
        return part.astype(jnp.bfloat16) if part.dtype == jnp.float32 else part

    return jax.tree.map(short, array)


def spread(value, axis, source):
    kept = jnp.where(lax.axis_index(axis) == source, value, 0).astype(value.dtype)
    return lax.psum(kept, axis)


def product_high(left, right):
    return jnp.dot(left, right, precision=lax.Precision.HIGHEST)


def inverse_transpose(top):
    blocks = PW // TILE
    identity = jnp.eye(TILE, dtype=jnp.float32)

    def tile_of(i, j):
        return top[i * TILE : (i + 1) * TILE, j * TILE : (j + 1) * TILE].astype(jnp.float32)

    def sym_tile(i, j):
        return 0.5 * (tile_of(i, j) + tile_of(j, i).T)

    lower = {}
    diag_inv = {}
    for j in range(blocks):
        accum = sym_tile(j, j)
        for k in range(j):
            accum = accum - product_high(lower[j, k], lower[j, k].T)
        lower[j, j] = jnp.linalg.cholesky(accum)
        diag_inv[j] = lax.linalg.triangular_solve(lower[j, j], identity, left_side=True, lower=True)
        for i in range(j + 1, blocks):
            accum = sym_tile(i, j)
            for k in range(j):
                accum = accum - product_high(lower[i, k], lower[j, k].T)
            lower[i, j] = product_high(accum, diag_inv[j].T)
    pieces = {}
    for i in range(blocks):
        pieces[i, i] = diag_inv[i]
    for i in range(blocks):
        for j in range(i):
            acc = jnp.zeros((TILE, TILE), jnp.float32)
            for k in range(j, i):
                acc = acc + product_high(lower[i, k], pieces[k, j])
            pieces[i, j] = -product_high(pieces[i, i], acc)
    zero_tile = jnp.zeros((TILE, TILE), jnp.bfloat16)
    row_list = [
        jnp.concatenate(
            [pieces[b, a].T.astype(jnp.bfloat16) if a <= b else zero_tile for b in range(blocks)],
            axis=1,
        )
        for a in range(blocks)
    ]
    return jnp.concatenate(row_list, axis=0)


def child_term(left_part, right_part):
    left_tiles = left_part.reshape(RANK, right_part.shape[0], TILE)
    result = jnp.einsum("rtk,trn->tkn", left_tiles, right_part, preferred_element_type=jnp.float32)
    return result.reshape(-1, TILE)


def shards(front, left_factors, right_factors):
    side = lax.axis_index("child")
    left_all = left_factors[0, 0]
    right_all = right_factors[0]
    update = lax.psum_scatter(
        child_term(left_all, right_all).astype(jnp.bfloat16),
        "child",
        scatter_dimension=0,
        tiled=True,
    ).astype(jnp.float32)
    panel_rows = (front.astype(jnp.float32) - update).astype(jnp.bfloat16)
    column = lax.axis_index("col")
    is_root = jnp.logical_and(side == 0, lax.axis_index("row") == 0)
    top = lax.all_gather(panel_rows[:PW], "col", axis=1, tiled=True)

    def select_block(matrix):
        return lax.dynamic_slice_in_dim(matrix, column * TILE, TILE, 0)

    empty_shape = (TILE, PW)
    local_block = lax.cond(
        is_root,
        lambda t: select_block(inverse_transpose(t)),
        lambda t: jnp.zeros(empty_shape, jnp.bfloat16),
        top,
    )
    inverse_block = jax.tree.map(
        lambda part, own: part.astype(own.dtype),
        jax.tree.map(lambda part: spread(part, ("child", "row"), 0), shortened(local_block)),
        local_block,
    )
    part = lax.slice_in_dim(inverse_block, 0, lax.axis_size("col") * TILE, axis=1)
    panel_t = lax.psum_scatter(
        lax.dot_general(
            part, panel_rows, (((0,), (1,)), ((), ())), preferred_element_type=jnp.float32
        ),
        "col",
        scatter_dimension=0,
        tiled=True,
    )
    return panel_t.astype(jnp.bfloat16)


def solution(mesh):
    in_specs = (
        P(("row", "child"), "col"),
        P("child", "col", None, "row"),
        P("child", "row", None, "col"),
    )
    out_specs = P("col", ("row", "child"))
    return jax.shard_map(shards, mesh=mesh, in_specs=in_specs, out_specs=out_specs, check_vma=False)
```

profile of v0, /device:TPU:1, one launch (start us, length us, event | category | flops | bytes accessed | tf_op | source)
XLA Modules:
  0.0 1288.6 jit_solution(6734739488787908376)
XLA Ops:
  6.5 1.3 copy.31
  7.8 0.0 copy-done
  7.8 0.0 copy-start.46
  7.8 3.2 convolution_convert_fusion
  11.1 0.0 reduce-scatter.3.cloned.1.call-update
  11.1 0.0 all-gather.2.cloned.1.call-start
  11.1 64.8 %reduce-scatter.3.cloned.1.call-done = bf16[2048,512]{1,0:T(8,128)(2,1)} async-done(((bf16[4096,512]{1,0:T(8,128)(2,1)}), bf16[2048,512]{1,0:T(8,128)(2,1)}) %reduce-scatter.3.cloned.1.call-update) | async-done | bytes 2097168 | tf_op jit(solution)/shard_map/reduce_scatter | solution.py:81
  76.0 3.5 subtract_convert_fusion
  79.5 0.0 all-gather.2.cloned.1.call-update
  79.5 0.0 all-reduce.4.cloned.1.call-start
  79.5 85.1 %all-gather.2.cloned.1.call-done = bf16[2048,2048]{1,0:T(8,128)(2,1)} async-done(((bf16[2048,512]{1,0:T(8,128)(2,1)}), bf16[2048,2048]{1,0:T(8,128)(2,1)}) %all-gather.2.cloned.1.call-update) | async-done | bytes 8388624 | tf_op jit(solution)/shard_map/all_gather | solution.py:90
  164.7 1.5 conditional.1
  164.7 1.5 broadcast.134
  166.2 1.5 broadcast_select_fusion
  167.7 0.0 all-reduce.4.cloned.1.call-update
  167.7 0.0 reduce-scatter.5.cloned.1.call-start
  167.8 949.7 %all-reduce.4.cloned.1.call-done = bf16[512,2048]{0,1:T(8,128)(2,1)} async-done(((bf16[512,2048]{0,1:T(8,128)(2,1)}), bf16[512,2048]{0,1:T(8,128)(2,1)}) %all-reduce.4.cloned.1.call-update) | async-done | bytes 2097168 | tf_op jit(solution)/shard_map/psum | solution.py:21
  1117.5 0.0 copy-done.35
  1117.5 9.7 fusion.185
  1127.2 0.0 reduce-scatter.5.cloned.1.call-update
  1127.2 0.0 copy-start.1
  1127.2 151.0 %reduce-scatter.5.cloned.1.call-done = f32[512,2048]{1,0:T(8,128)} async-done(((f32[2048,2048]{1,0:T(8,128)}), f32[512,2048]{1,0:T(8,128)}) %reduce-scatter.5.cloned.1.call-update) | async-done | bytes 4194320 | tf_op jit(solution)/shard_map/reduce_scatter | solution.py:108
  1278.2 3.8 convert_element_type.129
  1282.1 0.0 copy-done.1
  (4 shorter events, 0.0 us)
Async XLA Ops:
  6.5 1.3 copy-start
  6.5 69.4 %reduce-scatter.3.cloned.1.call-start = ((), (), s32[]{:S(2)}) async-start(), calls=%async_computation.2 | async-start | bytes 6291456 | tf_op jit(solution)/shard_map/reduce_scatter | solution.py:81
  7.8 68.1 %copy-start.46 = (bf16[2048,512]{1,0:T(8,128)(2,1)S(1)}, bf16[2048,512]{1,0:T(8,128)(2,1)}, u32[]{:S(2)}) copy-start(bf16[2048,512]{1,0:T(8,128)(2,1)} %param.8) | copy-start | bytes 6291460
  11.1 153.6 %all-gather.2.cloned.1.call-start = ((), (), s32[]{:S(2)}) async-start(), calls=%async_computation.3 | async-start | bytes 10485760 | tf_op jit(solution)/shard_map/all_gather | solution.py:90
  79.5 1038.0 %all-reduce.4.cloned.1.call-start = ((), (), s32[]{:S(2)}) async-start(), calls=%async_computation.4 | async-start | bytes 4194304 | tf_op jit(solution)/shard_map/psum | solution.py:21
  166.2 951.3 %copy-start.35 = (bf16[2048,512]{1,0:T(8,128)(2,1)S(1)}, bf16[2048,512]{1,0:T(8,128)(2,1)}, u32[]{:S(2)}) copy-start(bf16[2048,512]{1,0:T(8,128)(2,1)} %subtract_convert_fusion) | copy-start | bytes 6291460
  167.7 1110.5 %reduce-scatter.5.cloned.1.call-start = ((), (), s32[]{:S(2)}) async-start(), calls=%async_computation.5 | async-start | bytes 20971520 | tf_op jit(solution)/shard_map/reduce_scatter | solution.py:108
  1127.2 154.8 %copy-start.1 = (bf16[1,8,64,512]{3,2,1,0:T(8,128)(2,1)S(1)}, bf16[1,8,64,512]{3,2,1,0:T(8,128)(2,1)}, u32[]{:S(2)}) copy-start(bf16[1,8,64,512]{3,2,1,0:T(8,128)(2,1)} %param.10) | copy-start | bytes 1572868
Sparse Core Ops, SparseCore 0:
  11.2 64.6 reduce-scatter.2
  79.6 85.0 all-gather.1
  168.5 948.9 all-reduce.3
  1127.3 150.8 reduce-scatter.4
where the time goes:
time: 1290 us
  waiting for transfers between devices  1250 us (97%)
  between operations  13.2 us (1%)
  matrix products  12.9 us (1%)
    psum x1, waiting for transfers between devices, spread(): return lax.psum(kept, axis)  950 us
    reduce_scatter x1, waiting for transfers between devices, shards(): lax.psum_scatter(lax.dot_general(part, panel_rows, (((0,), (1,)), ((), ()...  151 us
    all_gather x1, waiting for transfers between devices, shards(): top = lax.all_gather(panel_rows[:PW], 'col', axis=1, tiled=True)  85.1 us
    reduce_scatter x1, waiting for transfers between devices, shards(): lax.psum_scatter(child_term(left_all, right_all).astype(jnp.bfloat16), 'c...  64.8 us
  transfers between devices with their start and end apart: 4, of which 4 were waited for; matrix products, arithmetic and copies ran while one was open for 0% of the time, Pallas kernels for 0%

commit v1 on v0

--- a/solution.py
+++ b/solution.py
@@ -87,7 +87,9 @@
     panel_rows = (front.astype(jnp.float32) - update).astype(jnp.bfloat16)
     column = lax.axis_index("col")
     is_root = jnp.logical_and(side == 0, lax.axis_index("row") == 0)
-    top = lax.all_gather(panel_rows[:PW], "col", axis=1, tiled=True)
+    top = jnp.concatenate(
+        lax.all_to_all(jnp.stack([panel_rows[:PW]] * lax.axis_size("col")), "col", 0, 0), axis=1
+    )
 
     def select_block(matrix):
         return lax.dynamic_slice_in_dim(matrix, column * TILE, TILE, 0)

time: 1290 us -> 1330 us (1.031)
  waiting for transfers between devices: 1250 us -> 1280 us
    all_to_all x0 -> x1, waiting for transfers between devices: none -> 93.1 us  [shards(): lax.all_to_all(jnp.stack([panel_rows[:PW]] * lax.axis_size('col')), 'col'...]
    all_gather x1 -> x0, waiting for transfers between devices: 85.1 us -> none  [shards(): top = lax.all_gather(panel_rows[:PW], 'col', axis=1, tiled=True)]
    psum x1, waiting for transfers between devices: 950 us -> 974 us  [spread(): return lax.psum(kept, axis)]
where the time goes in v1:
time: 1330 us
  waiting for transfers between devices  1280 us (96%)
    psum x1, waiting for transfers between devices, spread(): return lax.psum(kept, axis)  974 us
    reduce_scatter x1, waiting for transfers between devices, shards(): lax.psum_scatter(lax.dot_general(part, panel_rows, (((0,), (1,)), ((), ()...  151 us
    all_to_all x1, waiting for transfers between devices, shards(): lax.all_to_all(jnp.stack([panel_rows[:PW]] * lax.axis_size('col')), 'col'...  93.1 us
    reduce_scatter x1, waiting for transfers between devices, shards(): lax.psum_scatter(child_term(left_all, right_all).astype(jnp.bfloat16), 'c...  64.9 us
  transfers between devices with their start and end apart: 4, of which 4 were waited for; matrix products, arithmetic and copies ran while one was open for 0% of the time, Pallas kernels for 0%

profile of v1, /device:TPU:1, one launch (start us, length us, event | category | flops | bytes accessed | tf_op | source)
XLA Modules:
  0.0 1330.5 jit_solution(16687574312937381295)
XLA Ops:
  6.5 1.3 copy.109
  7.8 0.0 copy-done
  7.8 0.0 copy-start.43
  7.8 3.2 convolution_convert_fusion
  11.1 0.0 reduce-scatter.3.cloned.1.call-update
  11.1 64.9 %reduce-scatter.3.cloned.1.call-done = bf16[2048,512]{1,0:T(8,128)(2,1)} async-done(((bf16[4096,512]{1,0:T(8,128)(2,1)}), bf16[2048,512]{1,0:T(8,128)(2,1)}) %reduce-scatter.3.cloned.1.call-update) | async-done | bytes 2097168 | tf_op jit(solution)/shard_map/reduce_scatter | solution.py:81
  76.0 2.2 subtract_convert_fusion
  78.1 1.3 copy-done.31
  79.5 4.0 stack.2
  83.5 5.6 all-to-all-start
  89.1 0.0 all-reduce.4.cloned.1.call-start
  89.2 93.1 %all-to-all-done = bf16[4,2048,512]{2,1,0:T(8,128)(2,1)} async-done(((bf16[4,2048,512]{2,1,0:T(8,128)(2,1)}), bf16[4,2048,512]{2,1,0:T(8,128)(2,1)}, u32[]{:S(2)}, u32[]{:S(2)}) %all-to-all-start) | async-done | bytes 8388640 | tf_op jit(solution)/shard_map/all_to_all | solution.py:91
  182.3 1.5 conditional.1
  182.3 1.5 broadcast.136
  183.7 1.5 broadcast_select_fusion
  185.2 0.0 all-reduce.4.cloned.1.call-update
  185.2 0.0 reduce-scatter.5.cloned.1.call-start
  185.3 974.1 %all-reduce.4.cloned.1.call-done = bf16[512,2048]{0,1:T(8,128)(2,1)} async-done(((bf16[512,2048]{0,1:T(8,128)(2,1)}), bf16[512,2048]{0,1:T(8,128)(2,1)}) %all-reduce.4.cloned.1.call-update) | async-done | bytes 2097168 | tf_op jit(solution)/shard_map/psum | solution.py:21
  1159.4 9.7 fusion.181
  1169.1 0.0 reduce-scatter.5.cloned.1.call-update
  1169.1 0.0 copy-start.1
  1169.1 151.0 %reduce-scatter.5.cloned.1.call-done = f32[512,2048]{1,0:T(8,128)} async-done(((f32[2048,2048]{1,0:T(8,128)}), f32[512,2048]{1,0:T(8,128)}) %reduce-scatter.5.cloned.1.call-update) | async-done | bytes 4194320 | tf_op jit(solution)/shard_map/reduce_scatter | solution.py:110
  1320.1 3.8 convert_element_type.129
  1323.9 0.0 copy-done.1
  (6 shorter events, 0.0 us)
Async XLA Ops:
  6.5 1.3 copy-start
  6.5 69.4 %reduce-scatter.3.cloned.1.call-start = ((), (), s32[]{:S(2)}) async-start(), calls=%async_computation.3 | async-start | bytes 6291456 | tf_op jit(solution)/shard_map/reduce_scatter | solution.py:81
  7.8 68.1 %copy-start.43 = (bf16[2048,512]{1,0:T(8,128)(2,1)S(1)}, bf16[2048,512]{1,0:T(8,128)(2,1)}, u32[]{:S(2)}) copy-start(bf16[2048,512]{1,0:T(8,128)(2,1)} %param.8) | copy-start | bytes 6291460
  78.1 1.4 copy-start.31
  83.5 98.8 %all-to-all-start = ((bf16[4,2048,512]{2,1,0:T(8,128)(2,1)}), bf16[4,2048,512]{2,1,0:T(8,128)(2,1)}, u32[]{:S(2)}, u32[]{:S(2)}) async-start(bf16[4,2048,512]{2,1,0:T(8,128)(2,1)} %stack.2), calls=%async_computation.1 | async-start | bytes 16777216 | tf_op jit(solution)/shard_map/all_to_all | solution.py:91
  89.1 1070.3 %all-reduce.4.cloned.1.call-start = ((), (), s32[]{:S(2)}) async-start(), calls=%async_computation.4 | async-start | bytes 4194304 | tf_op jit(solution)/shard_map/psum | solution.py:21
  183.7 975.7 %copy-start.32 = (bf16[2048,512]{1,0:T(8,128)(2,1)S(1)}, bf16[2048,512]{1,0:T(8,128)(2,1)}, u32[]{:S(2)}) copy-start(bf16[2048,512]{1,0:T(8,128)(2,1)} %copy-done.31) | copy-start | bytes 6291460
  185.2 1134.9 %reduce-scatter.5.cloned.1.call-start = ((), (), s32[]{:S(2)}) async-start(), calls=%async_computation.5 | async-start | bytes 20971520 | tf_op jit(solution)/shard_map/reduce_scatter | solution.py:110
  1169.1 154.8 %copy-start.1 = (bf16[1,8,64,512]{3,2,1,0:T(8,128)(2,1)S(1)}, bf16[1,8,64,512]{3,2,1,0:T(8,128)(2,1)}, u32[]{:S(2)}) copy-start(bf16[1,8,64,512]{3,2,1,0:T(8,128)(2,1)} %param.10) | copy-start | bytes 1572868
Sparse Core Ops, SparseCore 0:
  11.2 64.6 reduce-scatter.2
  185.3 974.0 all-reduce.3
  1169.2 150.8 reduce-scatter.4
